TPU v7x, 512 devices: a whole 4x4x16 slice. The times are simulated.
512 devices in a mesh: row: 32 (over z, x_lo), rep: 16 (over x_hi, y, core).
Axes of the slice: x: 4 (x_hi: 2, x_lo: 2; x = x_hi * 2 + x_lo), y: 4, z: 16, core: 2. Of those that a mesh axis runs over, the one named last changes fastest.
Arguments:
- features: bfloat16 [131072, 256], P(('row', 'rep')), may hold values from -6 to 6
- dense_blocks: bfloat16 [131072, 2, 4096], P('row', None, 'rep'), may hold values from -0.0625 to 0.0625
- thick_neighbour_labels: int32 [32, 2], P('row'), may hold values from 0 to 31, as said below
- tile_source: int32 [32, 16, 64], P('row', 'rep'), may hold values from 0 to 63, as said below
- tile_dest: int32 [32, 16, 64], P('row', 'rep'), may hold values from 0 to 31
- entry_rows: int32 [32, 16, 64, 512], P('row', 'rep'), may hold values from 0 to 127, as said below
- entry_cols: int32 [32, 16, 64, 512], P('row', 'rep'), may hold values from 0 to 127
- edge_strength_list: bfloat16 [32, 16, 64, 512], P('row', 'rep'), may hold values from -0.75 to 0.75
- entry_count: int32 [32, 16, 64], P('row', 'rep'), may hold values from 1 to 512
- weight: bfloat16 [256, 256], replicated, may hold values from -0.375 to 0.375
- out_bias: float32 [256], replicated, may hold values from -3 to 3
Outputs:
- activated: bfloat16 [131072, 256], P(('row', 'rep'))
Inputs may be any that keep to these rules, and one draw needn't show every extreme that they name: `thick_neighbour_labels`: each row block's dense source blocks are distinct and lie within cyclic distance 3 of its own block id. Within one device's list, entries with the same source row block (tile_source // 2) name the same tile. The (entry_rows, entry_cols) pairs of one sparse tile's entries are distinct.
All inputs are finite; a program needn't handle non-finite values.
Results may differ from a plain program's by a relative error of at most 0.0047.
Values may be sent and summed in bfloat16 or wider, within the bound.
A program may use at most 64 MiB of HBM per device.

v0:
```python
import jax
import jax.numpy as jnp
from jax import lax
from jax.sharding import PartitionSpec as P

FEAT = 256
TILE = 128
TILES_DEV = 2


def sparse_terms(
    src_tiles, tile_dest, entry_rows, entry_cols, edge_strength_list, entry_count, dest_tiles
):
    entry_index = lax.broadcasted_iota(jnp.int32, entry_rows.shape, 1)
    active = entry_index < entry_count[:, None]
    weights_live = jnp.where(active, edge_strength_list.astype(jnp.float32), 0.0)
    positions = lax.broadcasted_iota(jnp.int32, (1, 1, TILE), 2)
    row_onehot = (entry_rows[:, :, None] == positions).astype(jnp.bfloat16)
    col_weighted = jnp.where(
        entry_cols[:, :, None] == positions, weights_live[:, :, None], 0.0
    ).astype(jnp.bfloat16)
    tile_mats = jnp.einsum(
        "snr,snc->src", row_onehot, col_weighted, preferred_element_type=jnp.float32
    ).astype(jnp.bfloat16)
    summand_piece = jnp.einsum(
        "src,scf->srf", tile_mats, src_tiles, preferred_element_type=jnp.float32
    )
    target_onehot_mask = (
        tile_dest[None, :] == lax.broadcasted_iota(jnp.int32, (dest_tiles, 1), 0)
    ).astype(jnp.float32)
    placed_entries = jnp.einsum(
        "ou,uwd->owd", target_onehot_mask, summand_piece, precision=lax.Precision.HIGHEST
    )
    return placed_entries.reshape(dest_tiles * TILE, summand_piece.shape[2])


def shards(
    features,
    dense_blocks,
    thick_neighbour_labels,
    tile_source,
    tile_dest,
    entry_rows,
    entry_cols,
    edge_strength_list,
    entry_count,
    weight,
    out_bias,
):
    row_count = lax.axis_size("row")
    own_rows = features.shape[0]
    block_rows = dense_blocks.shape[0]
    block_ids = thick_neighbour_labels[0]
    listed = tile_source[0, 0]
    gathered = lax.all_gather(features, "row", axis=0, tiled=True)
    panel_stack = gathered.reshape(row_count, own_rows, FEAT)
    dense_panels = panel_stack[block_ids]
    src_tiles = gathered.reshape(row_count * TILES_DEV, TILE, FEAT)[listed]
    sparse_part = sparse_terms(
        src_tiles,
        tile_dest[0, 0],
        entry_rows[0, 0],
        entry_cols[0, 0],
        edge_strength_list[0, 0],
        entry_count[0, 0],
        block_rows // TILE,
    )
    dense_part = jnp.einsum(
        "nsc,scf->nf", dense_blocks, dense_panels, preferred_element_type=jnp.float32
    )
    summed = lax.psum_scatter(dense_part + sparse_part, "rep", scatter_dimension=0, tiled=True)
    hidden = summed.astype(jnp.bfloat16)
    projected = jnp.dot(hidden, weight, preferred_element_type=jnp.float32) + out_bias
    return jnp.maximum(projected, 0.0).astype(jnp.bfloat16)


def solution(mesh):
    return jax.shard_map(
        shards,
        mesh=mesh,
        in_specs=(
            P(("row", "rep"), None),
            P("row", None, "rep"),
            P("row", None),
            P("row", "rep", None),
            P("row", "rep", None),
            P("row", "rep", None, None),
            P("row", "rep", None, None),
            P("row", "rep", None, None),
            P("row", "rep", None),
            P(),
            P(),
        ),
        out_specs=P(("row", "rep"), None),
        check_vma=False,
    )
```

profile of v0, /device:TPU:32, one launch (start us, length us, event | category | flops | bytes accessed | tf_op | source)
XLA Modules:
  0.0 315.6 jit_solution(13413633316712423619)
XLA Ops:
  6.5 0.0 copy-start
  6.5 0.0 all-gather.2.cloned.1.call-start
  6.5 0.7 all-gather.2.cloned.1.call-update
  7.3 0.0 reduce-scatter.2.cloned.1.call-start
  7.3 0.7 fusion.18
  8.0 0.7 fusion.17
  8.6 0.9 convert_select_fusion
  9.6 142.9 %all-gather.2.cloned.1.call-done = bf16[8192,256]{1,0:T(8,128)(2,1)} async-done(((bf16[256,256]{1,0:T(8,128)(2,1)}), bf16[8192,256]{1,0:T(8,128)(2,1)}) %all-gather.2.cloned.1.call-update) | async-done | bytes 4194320 | tf_op jit(solution)/shard_map/all_gather | solution.py:55
  152.5 0.0 copy-start.3
  152.5 0.0 copy-start.4
  152.5 5.0 %gather_fusion.1 = bf16[64,128,256]{2,1,0:T(8,128)(2,1)} fusion(bf16[64,128,256]{2,1,0:T(8,128)(2,1)} %bitcast.32, s32[1024]{0:T(1024)S(1)} %pad_clamp_fusion), kind=kCustom, calls=%fused_computation.1 | custom fusion | bytes 8388864 | tf_op jit(solution)/shard_map/gather | solution.py:58
  157.5 0.0 copy-done.3
  157.5 0.0 copy-done.4
  157.5 0.0 copy-start.2
  157.5 22.5 %fusion.9 = f32[64,128,256]{2,1,0:T(8,128)} fusion(bf16[64,128,256]{2,1,0:T(8,128)(2,1)} %gather_fusion.1, bf16[64,512]{1,0:T(8,128)(2,1)S(1)} %convert_select_fusion, s32[64,512]{1,0:T(8,128)S(1)} %bitcast.36, s32[64,512]{1,0:T(8,128)S(1)} %bitcast.37), kind=kOutput, calls=%fused_computation.15 | convolution fusion | flops 1624244224 | bytes 12910592 | tf_op jit(solution)/shard_map/src,scf->srf/dot_general | solution.py:25
  180.0 0.0 copy-done.2
  180.0 11.3 %fusion.1 = f32[32,128,256]{2,0,1:T(8,128)S(1)} fusion(f32[64,128,256]{2,1,0:T(8,128)} %fusion.9, s32[64]{0:T(128)S(1)} %bitcast.35), kind=kOutput, calls=%fused_computation.6 | convolution fusion | flops 805308416 | bytes 12583168 | tf_op jit(solution)/shard_map/ou,uwd->owd/dot_general | solution.py:31
  191.3 4.4 %copy.12 = f32[32,128,256]{2,1,0:T(8,128)} copy(f32[32,128,256]{2,0,1:T(8,128)S(1)} %fusion.1) | data formatting | bytes 8388608 | tf_op jit(solution)/shard_map/ou,uwd->owd/dot_general | solution.py:31
  195.7 2.7 gather_fusion
  198.4 6.7 %fusion.7 = f32[4096,256]{1,0:T(8,128)} fusion(f32[4096,256]{1,0:T(8,128)} %bitcast.31, bf16[2,256,256]{2,1,0:T(8,128)(2,1)S(1)} %gather_fusion, bf16[4096,2,256]{2,1,0:T(2,128)(2,1)} %param.12), kind=kOutput, calls=%fused_computation.13 | convolution fusion | flops 1074790400 | bytes 12845056 | tf_op jit(solution)/shard_map/nsc,scf->nf/dot_general | solution.py:68
  205.1 0.0 copy-start.1
  205.1 0.0 reduce-scatter.2.cloned.1.call-update
  205.1 101.8 %reduce-scatter.2.cloned.1.call-done = f32[256,256]{1,0:T(8,128)} async-done(((f32[4096,256]{1,0:T(8,128)}), f32[256,256]{1,0:T(8,128)}) %reduce-scatter.2.cloned.1.call-update) | async-done | bytes 262160 | tf_op jit(solution)/shard_map/reduce_scatter | solution.py:71
  307.0 0.0 copy-done
  307.0 0.0 copy-done.1
  307.0 1.8 fusion.12
  (2 shorter events, 0.0 us)
Async XLA Ops:
  6.5 300.4 %copy-start = (bf16[256,256]{1,0:T(8,128)(2,1)S(1)}, bf16[256,256]{1,0:T(8,128)(2,1)}, u32[]{:S(2)}) copy-start(bf16[256,256]{1,0:T(8,128)(2,1)} %param.20) | copy-start | bytes 393220
  6.5 146.0 %all-gather.2.cloned.1.call-start = ((), (), s32[]{:S(2)}) async-start(), calls=%async_computation.1 | async-start | bytes 4325376 | tf_op jit(solution)/shard_map/all_gather | solution.py:55
  7.3 299.7 %reduce-scatter.2.cloned.1.call-start = ((), (), s32[]{:S(2)}) async-start(), calls=%async_computation.2 | async-start | bytes 4456448 | tf_op jit(solution)/shard_map/reduce_scatter | solution.py:71
  152.5 5.0 %copy-start.3 = (s32[1,1,64,512]{3,2,1,0:T(8,128)S(1)}, s32[1,1,64,512]{3,2,1,0:T(8,128)}, u32[]{:S(2)}) copy-start(s32[1,1,64,512]{3,2,1,0:T(8,128)} %param.17) | copy-start | bytes 393220
  152.5 5.0 %copy-start.4 = (s32[1,1,64,512]{3,2,1,0:T(8,128)S(1)}, s32[1,1,64,512]{3,2,1,0:T(8,128)}, u32[]{:S(2)}) copy-start(s32[1,1,64,512]{3,2,1,0:T(8,128)} %param.16) | copy-start | bytes 393220
  157.5 22.5 %copy-start.2 = (s32[1,1,64]{2,1,0:T(1,128)S(1)}, s32[1,1,64]{2,1,0:T(1,128)}, u32[]{:S(2)}) copy-start(s32[1,1,64]{2,1,0:T(1,128)} %param.15) | copy-start | bytes 772
  205.1 101.8 %copy-start.1 = (f32[256]{0:T(256)S(1)}, f32[256]{0:T(256)}, u32[]{:S(2)}) copy-start(f32[256]{0:T(256)} %param.21) | copy-start | bytes 3076
Sparse Core Ops, SparseCore 0:
  9.4 143.0 all-gather.1
  205.3 101.6 reduce-scatter.1
where the time goes:
time: 316 us
  waiting for transfers between devices  245 us (78%)
  matrix products  42.3 us (13%)
  between operations  13.4 us (4%)
  local copies, waits for them, and re-layouts  12.1 us (4%)
    all_gather x1, waiting for transfers between devices, shards(): gathered = lax.all_gather(features, 'row', axis=0, tiled=True)  143 us
    reduce_scatter x1, waiting for transfers between devices, shards(): lax.psum_scatter(dense_part + sparse_part, 'rep', scatter_dimension=0, ti...  102 us
    dot_general x1, matrix products, sparse_terms(): jnp.einsum('src,scf->srf', tile_mats, src_tiles, preferred_element_type=j...  22.5 us
    dot_general x1, matrix products, sparse_terms(): jnp.einsum('ou,uwd->owd', target_onehot_mask, summand_piece, precision=la...  11.3 us
    dot_general x1, matrix products, shards(): jnp.einsum('nsc,scf->nf', dense_blocks, dense_panels, preferred_element_t...  6.71 us
  transfers between devices with their start and end apart: 2, of which 2 were waited for; matrix products, arithmetic and copies ran while one was open for 1% of the time, Pallas kernels for 0%

commit v1 on v0

--- a/solution.py
+++ b/solution.py
@@ -52,7 +52,9 @@
     block_rows = dense_blocks.shape[0]
     block_ids = thick_neighbour_labels[0]
     listed = tile_source[0, 0]
-    gathered = lax.all_gather(features, "row", axis=0, tiled=True)
+    gathered = jnp.concatenate(
+        lax.all_to_all(jnp.stack(lax.axis_size("row") * [features]), "row", 0, 0), axis=0
+    )
     panel_stack = gathered.reshape(row_count, own_rows, FEAT)
     dense_panels = panel_stack[block_ids]
     src_tiles = gathered.reshape(row_count * TILES_DEV, TILE, FEAT)[listed]

time: 316 us -> 374 us (1.18)
  waiting for transfers between devices: 245 us -> 285 us
  starting transfers between devices: 0.04 us -> 16.5 us
    all_to_all x0 -> x1, waiting for transfers between devices: none -> 187 us  [shards(): lax.all_to_all(jnp.stack(lax.axis_size('row') * [features]), 'row', 0, 0)]
    all_gather x1 -> x0, waiting for transfers between devices: 143 us -> none  [shards(): gathered = lax.all_gather(features, 'row', axis=0, tiled=True)]
    all_to_all x0 -> x1, starting transfers between devices: none -> 16.5 us  [shards(): lax.all_to_all(jnp.stack(lax.axis_size('row') * [features]), 'row', 0, 0)]
    reduce_scatter x1, waiting for transfers between devices: 102 us -> 98 us  [shards(): lax.psum_scatter(dense_part + sparse_part, 'rep', scatter_dimension=0, ti...]
  transfers between devices with their start and end apart: 2 -> 2, of which waited for: 2 -> 2; matrix products, arithmetic and copies ran while one was open for 1% -> 0% of each run, Pallas kernels for 0% -> 0%
where the time goes in v1:
time: 374 us; the launch traced here: 373 us
  waiting for transfers between devices  285 us (76%)
  matrix products  42.3 us (11%)
  starting transfers between devices  16.5 us (4%)
  local copies, waits for them, and re-layouts  15.5 us (4%)
  between operations  13.5 us (4%)
    all_to_all x1, waiting for transfers between devices, shards(): lax.all_to_all(jnp.stack(lax.axis_size('row') * [features]), 'row', 0, 0)  187 us
    reduce_scatter x1, waiting for transfers between devices, shards(): lax.psum_scatter(dense_part + sparse_part, 'rep', scatter_dimension=0, ti...  98 us
    dot_general x1, matrix products, sparse_terms(): jnp.einsum('src,scf->srf', tile_mats, src_tiles, preferred_element_type=j...  22.5 us
    all_to_all x1, starting transfers between devices, shards(): lax.all_to_all(jnp.stack(lax.axis_size('row') * [features]), 'row', 0, 0)  16.5 us
    dot_general x1, matrix products, sparse_terms(): jnp.einsum('ou,uwd->owd', target_onehot_mask, summand_piece, precision=la...  11.3 us
  transfers between devices with their start and end apart: 2, of which 2 were waited for; matrix products, arithmetic and copies ran while one was open for 0% of the time, Pallas kernels for 0%

profile of v1, /device:TPU:32, one launch (start us, length us, event | category | flops | bytes accessed | tf_op | source)
XLA Modules:
  0.0 373.3 jit_solution(7078012889984156031)
XLA Ops:
  6.5 0.0 copy-start
  6.5 3.4 stack.2
  9.9 0.0 copy-start.7
  9.9 0.0 copy-start.8
  9.9 0.0 copy-start.1
  9.9 0.0 copy-start.3
  9.9 16.5 %all-to-all-start = ((bf16[32,256,256]{2,1,0:T(8,128)(2,1)}), bf16[32,256,256]{2,1,0:T(8,128)(2,1)}, u32[]{:S(2)}, u32[]{:S(2)}) async-start(bf16[32,256,256]{2,1,0:T(8,128)(2,1)} %stack.2), calls=%async_computation | async-start | bytes 8388608 | tf_op jit(solution)/shard_map/all_to_all | solution.py:56
  26.4 0.0 reduce-scatter.2.cloned.1.call-start
  26.5 0.0 copy-done.7
  26.5 0.0 copy-done.8
  26.5 0.0 copy-done.1
  26.5 0.0 copy-done.3
  26.5 0.1 convert_select_fusion
  26.6 187.4 %all-to-all-done = bf16[32,256,256]{2,1,0:T(8,128)(2,1)} async-done(((bf16[32,256,256]{2,1,0:T(8,128)(2,1)}), bf16[32,256,256]{2,1,0:T(8,128)(2,1)}, u32[]{:S(2)}, u32[]{:S(2)}) %all-to-all-start) | async-done | bytes 4194336 | tf_op jit(solution)/shard_map/all_to_all | solution.py:56
  214.0 0.0 copy-start.5
  214.0 0.0 copy-start.6
  214.0 5.0 %gather_fusion.1 = bf16[64,128,256]{2,1,0:T(8,128)(2,1)} fusion(bf16[64,128,256]{2,1,0:T(8,128)(2,1)} %bitcast.10, s32[1024]{0:T(1024)S(1)} %pad_clamp_fusion), kind=kCustom, calls=%fused_computation.1 | custom fusion | bytes 8388864 | tf_op jit(solution)/shard_map/gather | solution.py:60
  219.0 0.0 copy-done.5
  219.0 0.0 copy-done.6
  219.0 0.0 copy-start.4
  219.0 22.5 %fusion.9 = f32[64,128,256]{2,1,0:T(8,128)} fusion(bf16[64,128,256]{2,1,0:T(8,128)(2,1)} %gather_fusion.1, bf16[64,512]{1,0:T(8,128)(2,1)S(1)} %convert_select_fusion, s32[64,512]{1,0:T(8,128)S(1)} %bitcast.33, s32[64,512]{1,0:T(8,128)S(1)} %bitcast.34), kind=kOutput, calls=%fused_computation.15 | convolution fusion | flops 1624244224 | bytes 12910592 | tf_op jit(solution)/shard_map/src,scf->srf/dot_general | solution.py:25
  241.5 0.0 copy-done.4
  241.5 11.3 %fusion.1 = f32[32,128,256]{2,0,1:T(8,128)S(1)} fusion(f32[64,128,256]{2,1,0:T(8,128)} %fusion.9, s32[64]{0:T(128)S(1)} %bitcast.32), kind=kOutput, calls=%fused_computation.6 | convolution fusion | flops 805308416 | bytes 12583168 | tf_op jit(solution)/shard_map/ou,uwd->owd/dot_general | solution.py:31
  252.8 4.4 %copy.12 = f32[32,128,256]{2,1,0:T(8,128)} copy(f32[32,128,256]{2,0,1:T(8,128)S(1)} %fusion.1) | data formatting | bytes 8388608 | tf_op jit(solution)/shard_map/ou,uwd->owd/dot_general | solution.py:31
  257.2 2.7 gather_fusion
  259.9 6.7 %fusion.7 = f32[4096,256]{1,0:T(8,128)} fusion(f32[4096,256]{1,0:T(8,128)} %bitcast.30, bf16[2,256,256]{2,1,0:T(8,128)(2,1)S(1)} %gather_fusion, bf16[4096,2,256]{2,1,0:T(2,128)(2,1)} %param.12), kind=kOutput, calls=%fused_computation.13 | convolution fusion | flops 1074790400 | bytes 12845056 | tf_op jit(solution)/shard_map/nsc,scf->nf/dot_general | solution.py:70
  266.6 0.0 copy-start.2
  266.6 0.0 reduce-scatter.2.cloned.1.call-update
  266.7 98.0 %reduce-scatter.2.cloned.1.call-done = f32[256,256]{1,0:T(8,128)} async-done(((f32[4096,256]{1,0:T(8,128)}), f32[256,256]{1,0:T(8,128)}) %reduce-scatter.2.cloned.1.call-update) | async-done | bytes 262160 | tf_op jit(solution)/shard_map/reduce_scatter | solution.py:73
  364.7 0.0 copy-done
  364.7 0.0 copy-done.2
  364.7 1.8 fusion.12
  (4 shorter events, 0.0 us)
Async XLA Ops:
  6.5 358.1 %copy-start = (bf16[256,256]{1,0:T(8,128)(2,1)S(1)}, bf16[256,256]{1,0:T(8,128)(2,1)}, u32[]{:S(2)}) copy-start(bf16[256,256]{1,0:T(8,128)(2,1)} %param.20) | copy-start | bytes 393220
  9.9 16.6 %copy-start.7 = (s32[1,1,64]{2,1,0:T(1,128)S(1)}, s32[1,1,64]{2,1,0:T(1,128)}, u32[]{:S(2)}) copy-start(s32[1,1,64]{2,1,0:T(1,128)} %param.14) | copy-start | bytes 772
  9.9 16.6 %copy-start.8 = (s32[1,2]{1,0:T(1,128)S(1)}, s32[1,2]{1,0:T(1,128)}, u32[]{:S(2)}) copy-start(s32[1,2]{1,0:T(1,128)} %param.13) | copy-start | bytes 28
  9.9 16.6 %copy-start.1 = (bf16[1,1,64,512]{3,2,1,0:T(8,128)(2,1)S(1)}, bf16[1,1,64,512]{3,2,1,0:T(8,128)(2,1)}, u32[]{:S(2)}) copy-start(bf16[1,1,64,512]{3,2,1,0:T(8,128)(2,1)} %param.18) | copy-start | bytes 196612
  9.9 16.6 %copy-start.3 = (s32[1,1,64]{2,1,0:T(1,128)S(1)}, s32[1,1,64]{2,1,0:T(1,128)}, u32[]{:S(2)}) copy-start(s32[1,1,64]{2,1,0:T(1,128)} %param.19) | copy-start | bytes 772
  9.9 204.1 %all-to-all-start = ((bf16[32,256,256]{2,1,0:T(8,128)(2,1)}), bf16[32,256,256]{2,1,0:T(8,128)(2,1)}, u32[]{:S(2)}, u32[]{:S(2)}) async-start(bf16[32,256,256]{2,1,0:T(8,128)(2,1)} %stack.2), calls=%async_computation | async-start | bytes 8388608 | tf_op jit(solution)/shard_map/all_to_all | solution.py:56
  26.4 338.3 %reduce-scatter.2.cloned.1.call-start = ((), (), s32[]{:S(2)}) async-start(), calls=%async_computation.2 | async-start | bytes 4456448 | tf_op jit(solution)/shard_map/reduce_scatter | solution.py:73
  214.0 5.0 %copy-start.5 = (s32[1,1,64,512]{3,2,1,0:T(8,128)S(1)}, s32[1,1,64,512]{3,2,1,0:T(8,128)}, u32[]{:S(2)}) copy-start(s32[1,1,64,512]{3,2,1,0:T(8,128)} %param.17) | copy-start | bytes 393220
  214.0 5.0 %copy-start.6 = (s32[1,1,64,512]{3,2,1,0:T(8,128)S(1)}, s32[1,1,64,512]{3,2,1,0:T(8,128)}, u32[]{:S(2)}) copy-start(s32[1,1,64,512]{3,2,1,0:T(8,128)} %param.16) | copy-start | bytes 393220
  219.0 22.5 %copy-start.4 = (s32[1,1,64]{2,1,0:T(1,128)S(1)}, s32[1,1,64]{2,1,0:T(1,128)}, u32[]{:S(2)}) copy-start(s32[1,1,64]{2,1,0:T(1,128)} %param.15) | copy-start | bytes 772
  266.6 98.1 %copy-start.2 = (f32[256]{0:T(256)S(1)}, f32[256]{0:T(256)}, u32[]{:S(2)}) copy-start(f32[256]{0:T(256)} %param.21) | copy-start | bytes 3076
Sparse Core Ops, SparseCore 0:
  266.8 97.8 reduce-scatter.1
